TPU v7x, 128 devices: a whole 4x4x4 slice. The times are simulated.
128 devices in a mesh: rep: 16 (over x, y), exp: 8 (over z, core).
Axes of the slice: x: 4, y: 4, z: 4, core: 2. Of those that a mesh axis runs over, the one named last changes fastest.
Arguments:
- hidden: bfloat16 [16384, 4096], P(('rep', 'exp')), may hold values from -6 to 6
- parents: int32 [16384], P(('rep', 'exp')), may hold values from 0 to 1023
- routes: int32 [16384, 8], P(('rep', 'exp')), may hold values from 0 to 127, all different within a row; in each aligned block of 128 rows (0 to 127, 128 to 255, ...) at most 10 rows name the same one
- gates: float32 [16384, 8], P(('rep', 'exp')), may hold values from 0.05 to 1
- counts: int32 [128], P(('rep', 'exp')), may hold values from 64 to 128, as said below
- norm_gain: float32 [4096], replicated, may hold values from 0.1 to 1.9
- w_gate: bfloat16 [128, 4096, 768], P(('rep', 'exp')), may hold values from -0.09375 to 0.09375
- w_up: bfloat16 [128, 4096, 768], P(('rep', 'exp')), may hold values from -0.09375 to 0.09375
- w_down: bfloat16 [128, 768, 4096], P(('rep', 'exp')), may hold values from -0.21875 to 0.21875
Outputs:
- mixed: bfloat16 [16384, 4096], P(('rep', 'exp'))
Inputs may be any that keep to these rules, and one draw needn't show every extreme that they name: `routes`: in the rows of one device no expert is named more than 10 times. `counts`: some device has all of its rows live.
All inputs are finite; a program needn't handle non-finite values.
Results may differ from a plain program's by a relative error of at most 0.0071.
Values may be sent and summed in bfloat16 or wider, within the bound.
A program may use at most 128 MiB of HBM per device.

v0:
```python
import jax
import jax.numpy as jnp
from jax import lax
from jax.sharding import PartitionSpec as P


def run_expert(arrived, w_gate, w_up, w_down):
    gate_val = jnp.dot(arrived, w_gate[0], preferred_element_type=jnp.float32)
    up_val = jnp.dot(arrived, w_up[0], preferred_element_type=jnp.float32)
    act = (jax.nn.silu(gate_val) * up_val).astype(jnp.bfloat16)
    return jnp.dot(act, w_down[0], preferred_element_type=jnp.float32).astype(jnp.bfloat16)


def shards(hidden, parents, routes, gates, counts, norm_gain, w_gate, w_up, w_down):
    rows = hidden.shape[0]
    width = hidden.shape[1]
    top = routes.shape[1]
    n_rep = lax.axis_size("rep")
    n_exp = lax.axis_size("exp")
    n_dev = n_rep * n_exp
    cap = rows * top // n_dev + 2
    column = lax.axis_index("exp")
    micro = rows * n_exp
    per_expert = cap * n_exp
    slots = n_rep * per_expert
    live = jnp.arange(rows, dtype=jnp.int32) < counts[0]
    weights = gates / jnp.sum(gates, axis=1, keepdims=True) * live[:, None].astype(jnp.float32)
    flat = routes.reshape(-1)
    live_slot = jnp.repeat(live, top)
    onehot = (
        (flat[:, None] == jnp.arange(n_dev, dtype=jnp.int32)[None, :]) & live_slot[:, None]
    ).astype(jnp.int32)
    before = jnp.cumsum(onehot, axis=0) - onehot
    rank = jnp.sum(before * onehot, axis=1)
    code = jnp.where(live_slot, flat, -1)
    ints = jnp.concatenate(
        [code.reshape(rows, top), rank.reshape(rows, top), parents[:, None]], axis=1
    )
    group = lax.all_gather(hidden, "exp", axis=0, tiled=True)
    ints_all = lax.all_gather(ints, "exp", axis=0, tiled=True)
    w_all = lax.all_gather(weights, "exp", axis=0, tiled=True)
    code_all = ints_all[:, :top]
    rank_all = ints_all[:, top : 2 * top]
    parent_all = ints_all[:, 2 * top]
    mine = (code_all >= 0) & (code_all % n_exp == column)
    owner = (jnp.arange(micro, dtype=jnp.int32) // rows)[:, None]
    dest = code_all // n_exp * per_expert + owner * cap + rank_all
    dest = jnp.where(mine, dest, slots).reshape(-1)
    row_id = jnp.broadcast_to(jnp.arange(micro, dtype=jnp.int32)[:, None], (micro, top)).reshape(-1)
    src_row = jnp.zeros((slots,), jnp.int32).at[dest].set(row_id, mode="drop")
    filled = jnp.zeros((slots,), jnp.bool_).at[dest].set(True, mode="drop")
    slot_w = jnp.zeros((slots,), jnp.float32).at[dest].set(w_all.reshape(-1), mode="drop")
    picked = jnp.take(group, jnp.take(parent_all, src_row), axis=0).astype(jnp.float32)
    scale = lax.rsqrt(jnp.mean(picked * picked, axis=1, keepdims=True) + 1e-06)
    normed = (picked * scale * norm_gain).astype(jnp.bfloat16)
    outgoing = jnp.where(filled[:, None], normed, jnp.zeros((), jnp.bfloat16))
    arrived = lax.all_to_all(outgoing, "rep", split_axis=0, concat_axis=0, tiled=True)
    results = run_expert(arrived, w_gate, w_up, w_down)
    returned = lax.all_to_all(results, "rep", split_axis=0, concat_axis=0, tiled=True)
    contrib = slot_w[:, None] * returned.astype(jnp.float32)
    target = jnp.where(filled, src_row, micro)
    partial = jnp.zeros((micro, width), jnp.float32).at[target].add(contrib, mode="drop")
    mixed = lax.psum_scatter(partial.astype(jnp.bfloat16), "exp", scatter_dimension=0, tiled=True)
    return mixed


def solution(mesh):
    placed = (
        P(("rep", "exp"), None),
        P(("rep", "exp")),
        P(("rep", "exp"), None),
        P(("rep", "exp"), None),
        P(("rep", "exp")),
        P(),
        P(("rep", "exp"), None, None),
        P(("rep", "exp"), None, None),
        P(("rep", "exp"), None, None),
    )
    return jax.shard_map(
        shards, mesh=mesh, in_specs=placed, out_specs=P(("rep", "exp"), None), check_vma=False
    )
```

profile of v0, /device:TPU:1, one launch (start us, length us, event | category | flops | bytes accessed | tf_op | source)
XLA Modules:
  0.0 590.4 jit_solution(2126128571061677138)
XLA Ops:
  6.5 0.7 all-gather.2.cloned.1.call-update
  7.3 0.8 copy.28
  9.2 0.3 fusion.17
  9.8 0.5 fusion.16
  10.4 0.7 broadcast_select_fusion
  11.1 0.7 pad_add_fusion
  11.8 15.3 %all_gather.9 = s32[1024,17]{0,1:T(8,128)S(1)} all-gather(s32[128,17]{0,1:T(8,128)S(1)} %pad_add_fusion), channel_id=1, replica_groups=mesh['rep'=16,'exp'=8] {'exp'}, dimensions={0}, use_global_device_ids=true | all-gather | bytes 78336 | tf_op jit(solution)/shard_map/all_gather | solution.py:40
  27.7 34.6 %scatter_custom_fusion = pred[1280]{0:T(1024)(128)(4,1)S(1)} fusion(s32[8192]{0:T(1024)S(1)} %bitcast.48, pred[8192]{0:T(1024)(128)(4,1)S(1)} %broadcast.149, pred[]{:T(512)} %constant.90.clone.1), kind=kCustom, calls=%fused_computation.72 | custom fusion | bytes 1281 | tf_op jit(solution)/shard_map/scatter | solution.py:51
  62.7 30.9 %scatter_custom_fusion.1 = s32[1280]{0:T(1024)S(1)} fusion(s32[8192]{0:T(1024)S(1)} %bitcast.49, s32[8192]{0:T(1024)S(1)} %reshape.182, s32[]{:T(128)} %constant.93.clone.1), kind=kCustom, calls=%fused_computation.69 | custom fusion | bytes 5124 | tf_op jit(solution)/shard_map/scatter | solution.py:50
  93.6 5.0 gather_fusion
  98.7 23.2 %gather_fusion.1 = bf16[1280,4096]{1,0:T(8,128)(2,1)} fusion(bf16[1024,4096]{1,0:T(8,128)(2,1)} %all-gather.2.cloned.1.call-done, s32[2048]{0:T(1024)S(1)} %pad_clamp_fusion), kind=kCustom, calls=%fused_computation.1 | custom fusion | bytes 20976640 | tf_op jit(solution)/shard_map/jit(_take)/gather | solution.py:53
  121.9 6.9 %multiply_reduce_fusion = f32[1280]{0:T(1024)S(1)} fusion(bf16[1280,4096]{1,0:T(8,128)(2,1)} %gather_fusion.1, pred[1280]{0:T(1024)(128)(4,1)S(1)} %get-tuple-element.5), kind=kLoop, calls=%fused_computation.9 | loop fusion | flops 20970240 | bytes 10492160 | tf_op jit(solution)/shard_map/reduce_sum | solution.py:54
  128.9 9.0 %fusion.1 = bf16[16,80,4096]{2,1,0:T(8,128)(2,1)S(1)} fusion(f32[4096]{0:T(1024)S(1)} %copy-done, f32[16,80]{1,0:T(8,128)S(1)} %rsqrt.12, bf16[16,80,4096]{2,1,0:T(8,128)(2,1)} %bitcast.44, pred[16,80]{1,0:T(8,128)(4,1)S(1)} %broadcast_in_dim.109, pred[16,80]{1,0:T(8,128)(4,1)S(1)} %broadcast_in_dim.105), kind=kLoop, calls=%fused_computation.11 | loop fusion | flops 31457280 | bytes 20995584 | tf_op jit(solution)/shard_map/jit(_where)/select_n | solution.py:56
  138.0 123.9 %all_to_all.18 = bf16[16,80,4096]{2,1,0:T(8,128)(2,1)S(1)} all-to-all(bf16[16,80,4096]{2,1,0:T(8,128)(2,1)S(1)} %fusion.1), channel_id=1, replica_groups=mesh['rep'=16,'exp'=8] {'rep'}, dimensions={0} | all-to-all | bytes 20971520 | tf_op jit(solution)/shard_map/all_to_all | solution.py:57
  261.9 11.8 %fusion.7 = f32[1280,768]{1,0:T(8,128)} fusion(bf16[1280,4096]{1,0:T(8,128)(2,1)S(1)} %bitcast.46, bf16[1,4096,768]{2,1,0:T(8,128)(2,1)} %param.15), kind=kOutput, calls=%fused_computation.17 | convolution fusion | flops 8053063680 | bytes 20709376 | tf_op jit(solution)/shard_map/dot_general | solution.py:8
  273.7 10.3 %fusion.12 = bf16[1280,768]{1,0:T(8,128)(2,1)S(1)} fusion(bf16[1280,4096]{1,0:T(8,128)(2,1)S(1)} %bitcast.47, bf16[1,4096,768]{2,1,0:T(8,128)(2,1)S(1)} %bitcast.53, f32[1280,768]{1,0:T(8,128)} %fusion.7), kind=kOutput, calls=%fused_computation.20 | convolution fusion | flops 8058961920 | bytes 22675456 | tf_op jit(solution)/shard_map/dot_general | solution.py:9
  284.1 10.7 %convolution_convert_fusion = bf16[1280,4096]{1,0:T(8,128)(2,1)} fusion(bf16[1280,768]{1,0:T(8,128)(2,1)S(1)} %fusion.12, bf16[1,768,4096]{2,1,0:T(8,128)(2,1)S(1)} %bitcast.55), kind=kOutput, calls=%fused_computation.10 | convolution fusion | flops 8058306560 | bytes 18743296 | tf_op jit(solution)/shard_map/dot_general | solution.py:11
  294.7 5.0 all-to-all-start.1
  299.8 14.9 %all_gather.10 = f32[1024,8]{0,1:T(8,128)S(1)} all-gather(f32[128,8]{0,1:T(8,128)S(1)} %divide_multiply_fusion), channel_id=1, replica_groups=mesh['rep'=16,'exp'=8] {'exp'}, dimensions={0}, use_global_device_ids=true | all-gather | bytes 36864 | tf_op jit(solution)/shard_map/all_gather | solution.py:41
  315.1 30.4 %scatter_custom_fusion.2 = f32[1280]{0:T(1024)S(1)} fusion(s32[8192]{0:T(1024)S(1)} %bitcast.50, f32[8192]{0:T(1024)S(1)} %reshape.190, f32[]{:T(128)} %constant.89.clone.1), kind=kCustom, calls=%fused_computation.67 | custom fusion | bytes 5124 | tf_op jit(solution)/shard_map/scatter | solution.py:52
  345.6 126.3 %all-to-all-done.1 = bf16[16,80,4096]{2,1,0:T(8,128)(2,1)} async-done(((bf16[16,80,4096]{2,1,0:T(8,128)(2,1)}), bf16[16,80,4096]{2,1,0:T(8,128)(2,1)}, u32[]{:S(2)}, u32[]{:S(2)}) %all-to-all-start.1) | async-done | bytes 10485792 | tf_op jit(solution)/shard_map/all_to_all | solution.py:59
  471.9 42.9 %scatter_custom_fusion.3 = f32[1024,4096]{1,0:T(8,128)} fusion(s32[1280]{0:T(1024)S(1)} %get-tuple-element.8, bf16[1280,4096]{1,0:T(8,128)(2,1)} %bitcast.16, f32[1280]{0:T(1024)S(1)} %scatter_custom_fusion.2, f32[]{:T(128)} %constant.89.clone.1), kind=kCustom, calls=%fused_computation.7 | custom fusion | flops 15728640 | bytes 27271172 | tf_op jit(solution)/shard_map/scatter-add | solution.py:62
  514.8 9.0 %convert_element_type.50 = bf16[1024,4096]{1,0:T(8,128)(2,1)} convert(f32[1024,4096]{1,0:T(8,128)} %scatter_custom_fusion.3) | non-fusion elementwise | flops 4194304 | bytes 25165824 | tf_op jit(solution)/shard_map/convert_element_type | solution.py:63
  523.8 59.5 %reduce-scatter.2.cloned.1.call-done = bf16[128,4096]{1,0:T(8,128)(2,1)} async-done(((bf16[1024,4096]{1,0:T(8,128)(2,1)}), bf16[128,4096]{1,0:T(8,128)(2,1)}) %reduce-scatter.2.cloned.1.call-update) | async-done | bytes 1048592 | tf_op jit(solution)/shard_map/reduce_scatter | solution.py:63
  (55 shorter events, 2.5 us)
Async XLA Ops:
  6.5 92.2 %all-gather.2.cloned.1.call-start = ((), (), s32[]{:S(2)}) async-start(), calls=%async_computation.3 | async-start | bytes 9437184 | tf_op jit(solution)/shard_map/all_gather | solution.py:39
  121.9 7.0 %copy-start = (f32[4096]{0:T(1024)S(1)}, f32[4096]{0:T(1024)}, u32[]{:S(2)}) copy-start(f32[4096]{0:T(1024)} %param.14) | copy-start | bytes 49156
  138.0 135.8 %slice-start = ((s8[6291456]{0:T(1024)(128)(4,1)}), s8[4194304]{0:T(1024)(128)(4,1)S(1)}, s32[]{:S(2)}) async-start(s8[6291456]{0:T(1024)(128)(4,1)} %bitcast.52), calls=%async_computation.5 | async-start | bytes 8388608
  138.0 146.1 %slice-start.2 = ((s8[6291456]{0:T(1024)(128)(4,1)}), s8[4194304]{0:T(1024)(128)(4,1)S(1)}, s32[]{:S(2)}) async-start(s8[6291456]{0:T(1024)(128)(4,1)} %bitcast.54), calls=%async_computation.7 | async-start | bytes 8388608
  261.9 11.8 %slice-start.1 = ((s8[6291456]{0:T(1024)(128)(4,1)}), s8[2097152]{0:T(1024)(128)(4,1)S(1)}, s32[]{:S(2)}) async-start(s8[6291456]{0:T(1024)(128)(4,1)} %bitcast.52), calls=%async_computation.6 | async-start | bytes 4194304
  261.9 22.2 %slice-start.3 = ((s8[6291456]{0:T(1024)(128)(4,1)}), s8[2097152]{0:T(1024)(128)(4,1)S(1)}, s32[]{:S(2)}) async-start(s8[6291456]{0:T(1024)(128)(4,1)} %bitcast.54), calls=%async_computation.8 | async-start | bytes 4194304
  294.7 5.0 copy-start.1
  294.7 177.1 %all-to-all-start.1 = ((bf16[16,80,4096]{2,1,0:T(8,128)(2,1)}), bf16[16,80,4096]{2,1,0:T(8,128)(2,1)}, u32[]{:S(2)}, u32[]{:S(2)}) async-start(bf16[16,80,4096]{2,1,0:T(8,128)(2,1)} %bitcast.45), calls=%async_computation.1 | async-start | bytes 20971520 | tf_op jit(solution)/shard_map/all_to_all | solution.py:59
  299.7 283.6 %reduce-scatter.2.cloned.1.call-start = ((), (), s32[]{:S(2)}) async-start(), calls=%async_computation.4 | async-start | bytes 9437184 | tf_op jit(solution)/shard_map/reduce_scatter | solution.py:63
Sparse Core Ops, SparseCore 0:
  9.1 53.5 all-gather.1
  523.9 59.3 reduce-scatter.1
where the time goes:
time: 597 us; the launch traced here: 590 us
  waiting for transfers between devices  187 us (31%)
  blocking collectives  154 us (26%)
  local copies, waits for them, and re-layouts  127 us (21%)
  other arithmetic  70.3 us (12%)
  matrix products  32.8 us (5%)
  between operations  14.6 us (2%)
    all_to_all x1, waiting for transfers between devices, shards(): lax.all_to_all(results, 'rep', split_axis=0, concat_axis=0, tiled=True)  126 us
    all_to_all x1, blocking collectives, shards(): lax.all_to_all(outgoing, 'rep', split_axis=0, concat_axis=0, tiled=True)  124 us
    reduce_scatter x1, waiting for transfers between devices, shards(): lax.psum_scatter(partial.astype(jnp.bfloat16), 'exp', scatter_dimension=0...  59.5 us
    scatter-add x1, other arithmetic, shards(): jnp.zeros((micro, width), jnp.float32).at[target].add(contrib, mode='drop')  42.9 us
    scatter x1, local copies, waits for them, and re-layouts, shards(): filled = jnp.zeros((slots,), jnp.bool_).at[dest].set(True, mode='drop')  34.6 us
    scatter x1, local copies, waits for them, and re-layouts, shards(): src_row = jnp.zeros((slots,), jnp.int32).at[dest].set(row_id, mode='drop')  30.9 us
    scatter x1, local copies, waits for them, and re-layouts, shards(): jnp.zeros((slots,), jnp.float32).at[dest]  30.4 us
    gather x1, local copies, waits for them, and re-layouts, shards(): jnp.take(group, jnp.take(parent_all, src_row), axis=0).astype(jnp.float32)  23.2 us
  transfers between devices with their start and end apart: 3, of which 2 were waited for; matrix products, arithmetic and copies ran while one was open for 18% of the time, Pallas kernels for 0%

commit v1 on v0

--- a/solution.py
+++ b/solution.py
@@ -56,7 +56,30 @@
     outgoing = jnp.where(filled[:, None], normed, jnp.zeros((), jnp.bfloat16))
     arrived = lax.all_to_all(outgoing, "rep", split_axis=0, concat_axis=0, tiled=True)
     results = run_expert(arrived, w_gate, w_up, w_down)
-    returned = lax.all_to_all(results, "rep", split_axis=0, concat_axis=0, tiled=True)
+
+    def process_unit(mine_x):
+        comm_axis = "rep"
+        big, block_out = (lax.axis_size(comm_axis), lax.axis_index(comm_axis))
+        even = list(mine_x.shape)
+        odd = mine_x.shape[0] // big
+        even[0] = odd
+        s_next = even[0]
+        even[0] = s_next * big
+        parts_out = jnp.zeros(even, mine_x.dtype)
+        for nth in range(big):
+            x_next = lax.dynamic_slice_in_dim(mine_x, (block_out ^ nth) * odd, odd, axis=0)
+            if nth:
+                x_next = lax.ppermute(
+                    x_next,
+                    axis_name=comm_axis,
+                    perm=list(map(lambda kk: (kk, kk ^ nth), range(big))),
+                )
+            parts_out = lax.dynamic_update_slice_in_dim(
+                parts_out, x_next, (block_out ^ nth) * s_next, axis=0
+            )
+        return parts_out
+
+    returned = process_unit(results)
     contrib = slot_w[:, None] * returned.astype(jnp.float32)
     target = jnp.where(filled, src_row, micro)
     partial = jnp.zeros((micro, width), jnp.float32).at[target].add(contrib, mode="drop")

time: 597 us -> 732 us (1.23)
  waiting for transfers between devices: 187 us -> 360 us
  blocking collectives: 154 us -> 29.9 us
  local copies, waits for them, and re-layouts: 127 us -> 159 us
  starting transfers between devices: 5.02 us -> 35 us
  other arithmetic: 70.3 us -> 91.1 us
    ppermute x0 -> x15, waiting for transfers between devices: none -> 130 us  [process_unit(): lax.ppermute(x_next, axis_name=comm_axis, perm=list(map(lambda kk: (kk, k...]
    all_to_all x1 -> x0, blocking collectives: 124 us -> none  [shards(): lax.all_to_all(outgoing, 'rep', split_axis=0, concat_axis=0, tiled=True)]
    all_to_all x1, waiting for transfers between devices: 126 us -> 179 us  [shards(): lax.all_to_all(outgoing, 'rep', split_axis=0, concat_axis=0, tiled=True)]
    ppermute x0 -> x15, starting transfers between devices: none -> 27.8 us  [process_unit(): lax.ppermute(x_next, axis_name=comm_axis, perm=list(map(lambda kk: (kk, k...]
    dynamic_update_slice x0 -> x15, local copies, waits for them, and re-layouts: none -> 15.6 us  [process_unit(): lax.dynamic_update_slice_in_dim(parts_out, x_next, (block_out ^ nth) * s_...]
    convert_element_type x0 -> x1, other arithmetic: none -> 13.9 us  [shards(): contrib = slot_w[:, None] * returned.astype(jnp.float32)]
    reduce_scatter x1, waiting for transfers between devices: 59.5 us -> 50 us  [shards(): lax.psum_scatter(partial.astype(jnp.bfloat16), 'exp', scatter_dimension=0...]
    mul x0 -> x1, local copies, waits for them, and re-layouts: none -> 8.38 us  [shards(): contrib = slot_w[:, None] * returned.astype(jnp.float32)]
  transfers between devices with their start and end apart: 3 -> 18, of which waited for: 2 -> 11; matrix products, arithmetic and copies ran while one was open for 18% -> 17% of each run, Pallas kernels for 0% -> 0%
where the time goes in v1:
time: 732 us; the launch traced here: 726 us
  waiting for transfers between devices  360 us (49%)
  local copies, waits for them, and re-layouts  159 us (22%)
  other arithmetic  91.1 us (12%)
  matrix products  35.2 us (5%)
  starting transfers between devices  35 us (5%)
  blocking collectives  29.9 us (4%)
  between operations  14.7 us (2%)
    all_to_all x1, waiting for transfers between devices, shards(): lax.all_to_all(outgoing, 'rep', split_axis=0, concat_axis=0, tiled=True)  179 us
    ppermute x15, waiting for transfers between devices, process_unit(): lax.ppermute(x_next, axis_name=comm_axis, perm=list(map(lambda kk: (kk, k...  130 us
    reduce_scatter x1, waiting for transfers between devices, shards(): lax.psum_scatter(partial.astype(jnp.bfloat16), 'exp', scatter_dimension=0...  50 us
    scatter-add x1, other arithmetic, shards(): jnp.zeros((micro, width), jnp.float32).at[target].add(contrib, mode='drop')  46.9 us
    scatter x1, local copies, waits for them, and re-layouts, shards(): filled = jnp.zeros((slots,), jnp.bool_).at[dest].set(True, mode='drop')  34.6 us
    scatter x1, local copies, waits for them, and re-layouts, shards(): src_row = jnp.zeros((slots,), jnp.int32).at[dest].set(row_id, mode='drop')  30.6 us
    scatter x1, local copies, waits for them, and re-layouts, shards(): jnp.zeros((slots,), jnp.float32).at[dest]  30.4 us
    ppermute x15, starting transfers between devices, process_unit(): lax.ppermute(x_next, axis_name=comm_axis, perm=list(map(lambda kk: (kk, k...  27.8 us
  transfers between devices with their start and end apart: 18, of which 11 were waited for; matrix products, arithmetic and copies ran while one was open for 17% of the time, Pallas kernels for 0%

profile of v1, /device:TPU:1, one launch (start us, length us, event | category | flops | bytes accessed | tf_op | source)
XLA Modules:
  0.0 725.6 jit_solution(3093043576242978220)
XLA Ops:
  11.8 15.3 %all_gather.9 = s32[1024,17]{0,1:T(8,128)S(1)} all-gather(s32[128,17]{0,1:T(8,128)S(1)} %pad_add_fusion), channel_id=1, replica_groups=mesh['rep'=16,'exp'=8] {'exp'}, dimensions={0}, use_global_device_ids=true | all-gather | bytes 78336 | tf_op jit(solution)/shard_map/all_gather | solution.py:40
  27.7 34.6 %scatter_custom_fusion = pred[1280]{0:T(1024)(128)(4,1)S(1)} fusion(s32[8192]{0:T(1024)S(1)} %bitcast.42, pred[8192]{0:T(1024)(128)(4,1)S(1)} %broadcast.155, pred[]{:T(512)} %constant.56.clone.1), kind=kCustom, calls=%fused_computation.102 | custom fusion | bytes 1281 | tf_op jit(solution)/shard_map/scatter | solution.py:51
  62.7 30.6 %scatter_custom_fusion.1 = s32[1280]{0:T(1024)S(1)} fusion(s32[8192]{0:T(1024)S(1)} %bitcast.43, s32[8192]{0:T(1024)S(1)} %reshape.177, s32[]{:T(128)} %constant.59.clone.1), kind=kCustom, calls=%fused_computation.99 | custom fusion | bytes 5124 | tf_op jit(solution)/shard_map/scatter | solution.py:50
  98.4 23.2 %gather_fusion.1 = bf16[1280,4096]{1,0:T(8,128)(2,1)} fusion(bf16[1024,4096]{1,0:T(8,128)(2,1)} %all-gather.2.cloned.1.call-done, s32[2048]{0:T(1024)S(1)} %pad_clamp_fusion), kind=kCustom, calls=%fused_computation.1 | custom fusion | bytes 20976640 | tf_op jit(solution)/shard_map/jit(_take)/gather | solution.py:53
  128.6 11.9 %fusion.2 = bf16[16,80,4096]{2,1,0:T(8,128)(2,1)} fusion(f32[4096]{0:T(1024)S(1)} %copy-done.2, f32[16,80]{1,0:T(8,128)S(1)} %rsqrt.12, bf16[16,80,4096]{2,1,0:T(8,128)(2,1)} %bitcast.41, pred[16,80]{1,0:T(8,128)(4,1)S(1)} %broadcast_in_dim.113, pred[16,80]{1,0:T(8,128)(4,1)S(1)} %broadcast_in_dim.109), kind=kLoop, calls=%fused_computation.11 | loop fusion | flops 31457280 | bytes 20995584 | tf_op jit(solution)/shard_map/jit(_where)/select_n | solution.py:56
  147.8 179.2 %all-to-all-done = bf16[16,80,4096]{2,1,0:T(8,128)(2,1)} async-done(((bf16[16,80,4096]{2,1,0:T(8,128)(2,1)}), bf16[16,80,4096]{2,1,0:T(8,128)(2,1)}, u32[]{:S(2)}, u32[]{:S(2)}) %all-to-all-start) | async-done | bytes 10485792 | tf_op jit(solution)/shard_map/all_to_all | solution.py:57
  327.0 12.3 %fusion.7 = f32[1280,768]{1,0:T(8,128)S(1)} fusion(bf16[1280,4096]{1,0:T(8,128)(2,1)} %bitcast.9, bf16[1,4096,768]{2,1,0:T(8,128)(2,1)} %param.15), kind=kOutput, calls=%fused_computation.16 | convolution fusion | flops 8053063680 | bytes 20709376 | tf_op jit(solution)/shard_map/dot_general | solution.py:8
  339.3 11.2 %fusion.12 = bf16[1280,768]{1,0:T(8,128)(2,1)S(1)} fusion(bf16[1280,4096]{1,0:T(8,128)(2,1)} %bitcast.9, bf16[1,4096,768]{2,1,0:T(8,128)(2,1)S(1)} %bitcast.47, f32[1280,768]{1,0:T(8,128)S(1)} %fusion.7), kind=kOutput, calls=%fused_computation.19 | convolution fusion | flops 8058961920 | bytes 22675456 | tf_op jit(solution)/shard_map/dot_general | solution.py:9
  350.5 11.7 %convolution_convert_fusion = bf16[1280,4096]{1,0:T(8,128)(2,1)S(1)} fusion(bf16[1280,768]{1,0:T(8,128)(2,1)S(1)} %fusion.12, bf16[1,768,4096]{2,1,0:T(8,128)(2,1)} %param.17), kind=kOutput, calls=%fused_computation.10 | convolution fusion | flops 8058306560 | bytes 18743296 | tf_op jit(solution)/shard_map/dot_general | solution.py:11
  374.6 14.6 %all_gather.10 = f32[1024,8]{0,1:T(8,128)S(1)} all-gather(f32[128,8]{0,1:T(8,128)S(1)} %divide_multiply_fusion), channel_id=1, replica_groups=mesh['rep'=16,'exp'=8] {'exp'}, dimensions={0}, use_global_device_ids=true | all-gather | bytes 36864 | tf_op jit(solution)/shard_map/all_gather | solution.py:41
  389.6 30.4 %scatter_custom_fusion.2 = f32[1280]{0:T(1024)S(1)} fusion(s32[8192]{0:T(1024)S(1)} %bitcast.44, f32[8192]{0:T(1024)S(1)} %reshape.185, f32[]{:T(128)} %constant.53.clone.1), kind=kCustom, calls=%fused_computation.97 | custom fusion | bytes 5124 | tf_op jit(solution)/shard_map/scatter | solution.py:52
  433.3 34.9 %collective-permute-done.2 = bf16[80,4096]{1,0:T(8,128)(2,1)S(1)} collective-permute-done((bf16[80,4096]{1,0:T(8,128)(2,1)}, bf16[80,4096]{1,0:T(8,128)(2,1)S(1)}, u32[]{:S(2)}, u32[]{:S(2)}) %collective-permute-start.2) | collective-permute-done | bytes 655392 | tf_op jit(solution)/shard_map/ppermute | solution.py:72
  474.5 10.7 %collective-permute-done.4 = bf16[80,4096]{1,0:T(8,128)(2,1)S(1)} collective-permute-done((bf16[80,4096]{1,0:T(8,128)(2,1)}, bf16[80,4096]{1,0:T(8,128)(2,1)S(1)}, u32[]{:S(2)}, u32[]{:S(2)}) %collective-permute-start.4) | collective-permute-done | bytes 655392 | tf_op jit(solution)/shard_map/ppermute | solution.py:72
  488.3 13.3 %collective-permute-done.5 = bf16[80,4096]{1,0:T(8,128)(2,1)S(1)} collective-permute-done((bf16[80,4096]{1,0:T(8,128)(2,1)}, bf16[80,4096]{1,0:T(8,128)(2,1)S(1)}, u32[]{:S(2)}, u32[]{:S(2)}) %collective-permute-start.5) | collective-permute-done | bytes 655392 | tf_op jit(solution)/shard_map/ppermute | solution.py:72
  504.8 10.4 %collective-permute-done.6 = bf16[80,4096]{1,0:T(8,128)(2,1)S(1)} collective-permute-done((bf16[80,4096]{1,0:T(8,128)(2,1)}, bf16[80,4096]{1,0:T(8,128)(2,1)S(1)}, u32[]{:S(2)}, u32[]{:S(2)}) %collective-permute-start.6) | collective-permute-done | bytes 655392 | tf_op jit(solution)/shard_map/ppermute | solution.py:72
  517.7 11.6 %collective-permute-done.7 = bf16[80,4096]{1,0:T(8,128)(2,1)S(1)} collective-permute-done((bf16[80,4096]{1,0:T(8,128)(2,1)}, bf16[80,4096]{1,0:T(8,128)(2,1)S(1)}, u32[]{:S(2)}, u32[]{:S(2)}) %collective-permute-start.7) | collective-permute-done | bytes 655392 | tf_op jit(solution)/shard_map/ppermute | solution.py:72
  532.2 12.1 %collective-permute-done.8 = bf16[80,4096]{1,0:T(8,128)(2,1)S(1)} collective-permute-done((bf16[80,4096]{1,0:T(8,128)(2,1)}, bf16[80,4096]{1,0:T(8,128)(2,1)S(1)}, u32[]{:S(2)}, u32[]{:S(2)}) %collective-permute-start.8) | collective-permute-done | bytes 655392 | tf_op jit(solution)/shard_map/ppermute | solution.py:72
  546.2 12.2 %collective-permute-done.9 = bf16[80,4096]{1,0:T(8,128)(2,1)S(1)} collective-permute-done((bf16[80,4096]{1,0:T(8,128)(2,1)}, bf16[80,4096]{1,0:T(8,128)(2,1)S(1)}, u32[]{:S(2)}, u32[]{:S(2)}) %collective-permute-start.9) | collective-permute-done | bytes 655392 | tf_op jit(solution)/shard_map/ppermute | solution.py:72
  560.8 11.6 %collective-permute-done.10 = bf16[80,4096]{1,0:T(8,128)(2,1)S(1)} collective-permute-done((bf16[80,4096]{1,0:T(8,128)(2,1)S(1)}, bf16[80,4096]{1,0:T(8,128)(2,1)S(1)}, u32[]{:S(2)}, u32[]{:S(2)}) %collective-permute-start.10) | collective-permute-done | bytes 655392 | tf_op jit(solution)/shard_map/ppermute | solution.py:72
  573.2 13.6 %collective-permute-done.11 = bf16[80,4096]{1,0:T(8,128)(2,1)S(1)} collective-permute-done((bf16[80,4096]{1,0:T(8,128)(2,1)S(1)}, bf16[80,4096]{1,0:T(8,128)(2,1)S(1)}, u32[]{:S(2)}, u32[]{:S(2)}) %collective-permute-start.11) | collective-permute-done | bytes 655392 | tf_op jit(solution)/shard_map/ppermute | solution.py:72
  590.4 13.9 %convert_element_type.45 = f32[1280,4096]{1,0:T(8,128)} convert(bf16[1280,4096]{1,0:T(8,128)(2,1)} %constant_dynamic-update-slice_fusion.14) | non-fusion elementwise | flops 5242880 | bytes 31457280 | tf_op jit(solution)/shard_map/convert_element_type | solution.py:83
  612.7 46.9 %scatter_custom_fusion.3 = f32[1024,4096]{1,0:T(8,128)} fusion(s32[1280]{0:T(1024)S(1)} %get-tuple-element.24, f32[1280,4096]{1,0:T(8,128)} %mul.135, f32[1280,4096]{1,0:T(8,128)} %convert_element_type.45, f32[]{:T(128)} %constant.53.clone.1), kind=kCustom, calls=%fused_computation.6 | custom fusion | flops 10485760 | bytes 58720260 | tf_op jit(solution)/shard_map/scatter-add | solution.py:85
  659.5 9.0 %convert_element_type.46 = bf16[1024,4096]{1,0:T(8,128)(2,1)} convert(f32[1024,4096]{1,0:T(8,128)} %scatter_custom_fusion.3) | non-fusion elementwise | flops 4194304 | bytes 25165824 | tf_op jit(solution)/shard_map/convert_element_type | solution.py:86
  668.6 50.0 %reduce-scatter.2.cloned.1.call-done = bf16[128,4096]{1,0:T(8,128)(2,1)} async-done(((bf16[1024,4096]{1,0:T(8,128)(2,1)}), bf16[128,4096]{1,0:T(8,128)(2,1)}) %reduce-scatter.2.cloned.1.call-update) | async-done | bytes 1048592 | tf_op jit(solution)/shard_map/reduce_scatter | solution.py:86
  (102 shorter events, 85.7 us)
Async XLA Ops:
  6.5 91.9 %all-gather.2.cloned.1.call-start = ((), (), s32[]{:S(2)}) async-start(), calls=%async_computation.2 | async-start | bytes 9437184 | tf_op jit(solution)/shard_map/all_gather | solution.py:39
  121.6 7.0 copy-start.2
  140.5 198.8 %slice-start = ((s8[6291456]{0:T(1024)(128)(4,1)}), s8[2097152]{0:T(1024)(128)(4,1)S(1)}, s32[]{:S(2)}) async-start(s8[6291456]{0:T(1024)(128)(4,1)} %bitcast.46), calls=%async_computation.4 | async-start | bytes 4194304
  140.5 186.5 %all-to-all-start = ((bf16[16,80,4096]{2,1,0:T(8,128)(2,1)}), bf16[16,80,4096]{2,1,0:T(8,128)(2,1)}, u32[]{:S(2)}, u32[]{:S(2)}) async-start(bf16[16,80,4096]{2,1,0:T(8,128)(2,1)} %fusion.2), calls=%async_computation | async-start | bytes 20971520 | tf_op jit(solution)/shard_map/all_to_all | solution.py:57
  147.4 571.2 %reduce-scatter.2.cloned.1.call-start = ((), (), s32[]{:S(2)}) async-start(), calls=%async_computation.3 | async-start | bytes 9437184 | tf_op jit(solution)/shard_map/reduce_scatter | solution.py:86
  327.0 12.3 %slice-start.1 = ((s8[6291456]{0:T(1024)(128)(4,1)}), s8[4194304]{0:T(1024)(128)(4,1)S(1)}, s32[]{:S(2)}) async-start(s8[6291456]{0:T(1024)(128)(4,1)} %bitcast.46), calls=%async_computation.5 | async-start | bytes 8388608
  367.5 6.9 copy-start.3
  370.9 54.4 %collective-permute-start = (bf16[80,4096]{1,0:T(8,128)(2,1)}, bf16[80,4096]{1,0:T(8,128)(2,1)}, u32[]{:S(2)}, u32[]{:S(2)}) collective-permute-start(bf16[80,4096]{1,0:T(8,128)(2,1)} %get-tuple-element.21), channel_id=1, source_target_pairs={{0,8},{8,0},{16,24},{24,16},{32,40},{40,32},{48,56},{56,48},{64,72... | collective-permute-start | bytes 1966088 | tf_op jit(solution)/shard_map/ppermute | solution.py:72
  374.5 55.1 %collective-permute-start.1 = (bf16[80,4096]{1,0:T(8,128)(2,1)}, bf16[80,4096]{1,0:T(8,128)(2,1)}, u32[]{:S(2)}, u32[]{:S(2)}) collective-permute-start(bf16[80,4096]{1,0:T(8,128)(2,1)} %get-tuple-element.20), channel_id=1, source_target_pairs={{0,16},{8,24},{16,0},{24,8},{32,48},{40,56},{48,32},{56,40},{64,80... | collective-permute-start | bytes 1966088 | tf_op jit(solution)/shard_map/ppermute | solution.py:72
  389.6 168.8 %copy-start = (bf16[80,4096]{1,0:T(8,128)(2,1)S(1)}, bf16[80,4096]{1,0:T(8,128)(2,1)}, u32[]{:S(2)}) copy-start(bf16[80,4096]{1,0:T(8,128)(2,1)} %get-tuple-element.10) | copy-start | bytes 1966084
  420.1 124.1 %copy-start.1 = (bf16[80,4096]{1,0:T(8,128)(2,1)S(1)}, bf16[80,4096]{1,0:T(8,128)(2,1)}, u32[]{:S(2)}) copy-start(bf16[80,4096]{1,0:T(8,128)(2,1)} %get-tuple-element.11) | copy-start | bytes 1966084
  420.1 169.4 %collective-permute-start.14 = (bf16[80,4096]{1,0:T(8,128)(2,1)S(1)}, bf16[80,4096]{1,0:T(8,128)(2,1)S(1)}, u32[]{:S(2)}, u32[]{:S(2)}) collective-permute-start(bf16[80,4096]{1,0:T(8,128)(2,1)S(1)} %get-tuple-element.7), channel_id=1, source_target_pairs={{0,120},{8,112},{16,104},{24,96},{32,88},{40,80},{48,72},{56,64},{... | collective-permute-start | bytes 1966088 | tf_op jit(solution)/shard_map/ppermute | solution.py:72
  420.2 168.4 %collective-permute-start.13 = (bf16[80,4096]{1,0:T(8,128)(2,1)S(1)}, bf16[80,4096]{1,0:T(8,128)(2,1)S(1)}, u32[]{:S(2)}, u32[]{:S(2)}) collective-permute-start(bf16[80,4096]{1,0:T(8,128)(2,1)S(1)} %get-tuple-element.8), channel_id=1, source_target_pairs={{0,112},{8,120},{16,96},{24,104},{32,80},{40,88},{48,64},{56,72},{... | collective-permute-start | bytes 1966088 | tf_op jit(solution)/shard_map/ppermute | solution.py:72
  423.8 163.9 %collective-permute-start.12 = (bf16[80,4096]{1,0:T(8,128)(2,1)S(1)}, bf16[80,4096]{1,0:T(8,128)(2,1)S(1)}, u32[]{:S(2)}, u32[]{:S(2)}) collective-permute-start(bf16[80,4096]{1,0:T(8,128)(2,1)S(1)} %get-tuple-element.9), channel_id=1, source_target_pairs={{0,104},{8,96},{16,120},{24,112},{32,72},{40,64},{48,88},{56,80},{... | collective-permute-start | bytes 1966088 | tf_op jit(solution)/shard_map/ppermute | solution.py:72
  425.3 42.9 %collective-permute-start.2 = (bf16[80,4096]{1,0:T(8,128)(2,1)}, bf16[80,4096]{1,0:T(8,128)(2,1)S(1)}, u32[]{:S(2)}, u32[]{:S(2)}) collective-permute-start(bf16[80,4096]{1,0:T(8,128)(2,1)} %get-tuple-element.19), channel_id=1, source_target_pairs={{0,24},{8,16},{16,8},{24,0},{32,56},{40,48},{48,40},{56,32},{64,88... | collective-permute-start | bytes 1966088 | tf_op jit(solution)/shard_map/ppermute | solution.py:72
  429.6 39.7 %collective-permute-start.3 = (bf16[80,4096]{1,0:T(8,128)(2,1)}, bf16[80,4096]{1,0:T(8,128)(2,1)S(1)}, u32[]{:S(2)}, u32[]{:S(2)}) collective-permute-start(bf16[80,4096]{1,0:T(8,128)(2,1)} %get-tuple-element.18), channel_id=1, source_target_pairs={{0,32},{8,40},{16,48},{24,56},{32,0},{40,8},{48,16},{56,24},{64,96... | collective-permute-start | bytes 1966088 | tf_op jit(solution)/shard_map/ppermute | solution.py:72
  468.2 16.9 %collective-permute-start.4 = (bf16[80,4096]{1,0:T(8,128)(2,1)}, bf16[80,4096]{1,0:T(8,128)(2,1)S(1)}, u32[]{:S(2)}, u32[]{:S(2)}) collective-permute-start(bf16[80,4096]{1,0:T(8,128)(2,1)} %get-tuple-element.17), channel_id=1, source_target_pairs={{0,40},{8,32},{16,56},{24,48},{32,8},{40,0},{48,24},{56,16},{64,10... | collective-permute-start | bytes 1966088 | tf_op jit(solution)/shard_map/ppermute | solution.py:72
  469.3 32.4 %collective-permute-start.5 = (bf16[80,4096]{1,0:T(8,128)(2,1)}, bf16[80,4096]{1,0:T(8,128)(2,1)S(1)}, u32[]{:S(2)}, u32[]{:S(2)}) collective-permute-start(bf16[80,4096]{1,0:T(8,128)(2,1)} %get-tuple-element.16), channel_id=1, source_target_pairs={{0,48},{8,56},{16,32},{24,40},{32,16},{40,24},{48,0},{56,8},{64,11... | collective-permute-start | bytes 1966088 | tf_op jit(solution)/shard_map/ppermute | solution.py:72
  485.2 30.1 %collective-permute-start.6 = (bf16[80,4096]{1,0:T(8,128)(2,1)}, bf16[80,4096]{1,0:T(8,128)(2,1)S(1)}, u32[]{:S(2)}, u32[]{:S(2)}) collective-permute-start(bf16[80,4096]{1,0:T(8,128)(2,1)} %get-tuple-element.15), channel_id=1, source_target_pairs={{0,56},{8,48},{16,40},{24,32},{32,24},{40,16},{48,8},{56,0},{64,12... | collective-permute-start | bytes 1966088 | tf_op jit(solution)/shard_map/ppermute | solution.py:72
  501.6 27.7 %collective-permute-start.7 = (bf16[80,4096]{1,0:T(8,128)(2,1)}, bf16[80,4096]{1,0:T(8,128)(2,1)S(1)}, u32[]{:S(2)}, u32[]{:S(2)}) collective-permute-start(bf16[80,4096]{1,0:T(8,128)(2,1)} %get-tuple-element.14), channel_id=1, source_target_pairs={{0,64},{8,72},{16,80},{24,88},{32,96},{40,104},{48,112},{56,120},{... | collective-permute-start | bytes 1966088 | tf_op jit(solution)/shard_map/ppermute | solution.py:72
  515.3 28.9 %collective-permute-start.8 = (bf16[80,4096]{1,0:T(8,128)(2,1)}, bf16[80,4096]{1,0:T(8,128)(2,1)S(1)}, u32[]{:S(2)}, u32[]{:S(2)}) collective-permute-start(bf16[80,4096]{1,0:T(8,128)(2,1)} %get-tuple-element.13), channel_id=1, source_target_pairs={{0,72},{8,64},{16,88},{24,80},{32,104},{40,96},{48,120},{56,112},{... | collective-permute-start | bytes 1966088 | tf_op jit(solution)/shard_map/ppermute | solution.py:72
  529.3 29.1 %collective-permute-start.9 = (bf16[80,4096]{1,0:T(8,128)(2,1)}, bf16[80,4096]{1,0:T(8,128)(2,1)S(1)}, u32[]{:S(2)}, u32[]{:S(2)}) collective-permute-start(bf16[80,4096]{1,0:T(8,128)(2,1)} %get-tuple-element.12), channel_id=1, source_target_pairs={{0,80},{8,88},{16,64},{24,72},{32,112},{40,120},{48,96},{56,104},{... | collective-permute-start | bytes 1966088 | tf_op jit(solution)/shard_map/ppermute | solution.py:72
  544.2 28.1 %collective-permute-start.10 = (bf16[80,4096]{1,0:T(8,128)(2,1)S(1)}, bf16[80,4096]{1,0:T(8,128)(2,1)S(1)}, u32[]{:S(2)}, u32[]{:S(2)}) collective-permute-start(bf16[80,4096]{1,0:T(8,128)(2,1)S(1)} %copy-done.1), channel_id=1, source_target_pairs={{0,88},{8,80},{16,72},{24,64},{32,120},{40,112},{48,104},{56,96},{... | collective-permute-start | bytes 1966088 | tf_op jit(solution)/shard_map/ppermute | solution.py:72
  558.4 28.4 %collective-permute-start.11 = (bf16[80,4096]{1,0:T(8,128)(2,1)S(1)}, bf16[80,4096]{1,0:T(8,128)(2,1)S(1)}, u32[]{:S(2)}, u32[]{:S(2)}) collective-permute-start(bf16[80,4096]{1,0:T(8,128)(2,1)S(1)} %copy-done), channel_id=1, source_target_pairs={{0,96},{8,104},{16,112},{24,120},{32,64},{40,72},{48,80},{56,88},{... | collective-permute-start | bytes 1966088 | tf_op jit(solution)/shard_map/ppermute | solution.py:72
Sparse Core Ops, SparseCore 0:
  9.1 53.5 all-gather.1
  668.7 49.8 reduce-scatter.1
